TPU v7x, 512 devices: a whole 4x8x8 slice. The times are simulated.
512 devices in a mesh: row: 16 (over y, core), col: 32 (over z, x).
Axes of the slice: x: 4, y: 8, z: 8, core: 2. Of those that a mesh axis runs over, the one named last changes fastest.
Arguments:
- child_vectors: bfloat16 [2, 8192, 65536], P(None, 'row', 'col'), may hold values from -6 to 6
- merge_position: int32 [2, 65536], P(None, 'col'), may hold values from 0 to 131071, as said below
- pole_frac: float32 [2, 65536], P(None, 'col'), may hold values from 0 to 0.3
- weights: float32 [2, 65536], P(None, 'col'), may hold values from -3 to 3, as said below
- retained: int32 [2, 65536], P(None, 'col'), may hold values from 0 to 1, as said below
- root_index: int32 [512], replicated, may hold values from 0 to 131070
- root_offset: float32 [512], replicated, may hold values from 0.55 to 0.75
Outputs:
- merged: bfloat16 [2, 8192, 512], P(None, ('row', 'col'))
Inputs may be any that keep to these rules, and one draw needn't show every extreme that they name: `merge_position`: each merged position 0 to 131071 occurs exactly once over both children. The first pole of each aligned block of 2048 poles of a child is retained; elsewhere whole aligned blocks of 512 poles may be deflated. `weights`: magnitudes lie between 0.3 and 3.
All inputs are finite; a program needn't handle non-finite values.
Results may differ from a plain program's by a relative error of at most 0.015.
Values may be sent and summed in bfloat16 or wider, within the bound.
A program may use at most 64 MiB of HBM per device.

v0:
```python
import jax
import jax.numpy as jnp
from jax import lax
from jax.sharding import PartitionSpec as P

PANEL = 128


def local(child_vectors, merge_position, pole_frac, weights, retained, root_index, root_offset):
    half_local = child_vectors.shape[2]
    share_rows = half_local // lax.axis_size("row")
    offset_rows = lax.axis_index("row") * share_rows
    position = lax.dynamic_slice_in_dim(merge_position, offset_rows, share_rows, 1)
    fraction = lax.dynamic_slice_in_dim(pole_frac, offset_rows, share_rows, 1)
    weight = lax.dynamic_slice_in_dim(weights, offset_rows, share_rows, 1)
    keep_mask = lax.dynamic_slice_in_dim(retained, offset_rows, share_rows, 1)
    scaled = keep_mask.astype(jnp.float32) * weight
    panel_count = root_index.shape[0] // PANEL
    results = []
    for number in range(panel_count):
        first_col = number * PANEL
        root_rows = root_index[first_col : first_col + PANEL]
        root_parts = root_offset[first_col : first_col + PANEL]
        spacing = (position[:, :, None] - root_rows[None, None, :]).astype(jnp.float32) + (
            fraction[:, :, None] - root_parts[None, None, :]
        )
        raw_panel = scaled[:, :, None] / spacing
        squares = jnp.sum(raw_panel * raw_panel, axis=(0, 1))
        panel_block = (
            raw_panel * lax.rsqrt(lax.psum(squares, ("row", "col")))[None, None, :]
        ).astype(jnp.bfloat16)
        panel_block = lax.all_gather(panel_block, "row", axis=1, tiled=True)
        partial_value = jnp.einsum(
            "crh,chm->crm", child_vectors, panel_block, preferred_element_type=jnp.float32
        )
        results.append(
            lax.psum_scatter(
                partial_value.astype(jnp.bfloat16), "col", scatter_dimension=1, tiled=True
            )
        )
    return jnp.concatenate(results, axis=2)


def solution(mesh):
    return jax.shard_map(
        local,
        mesh=mesh,
        in_specs=(
            P(None, "row", "col"),
            P(None, "col"),
            P(None, "col"),
            P(None, "col"),
            P(None, "col"),
            P(),
            P(),
        ),
        out_specs=P(None, ("row", "col"), None),
        check_vma=False,
    )
```

profile of v0, /device:TPU:56, one launch (start us, length us, event | category | flops | bytes accessed | tf_op | source)
XLA Modules:
  0.0 448.7 jit_solution(2952448163748329389)
XLA Ops:
  6.5 0.0 copy-start
  6.5 0.0 all-gather.7.cloned.1.call-start
  6.5 0.8 fusion.4
  7.4 0.8 fusion.5
  8.2 0.0 copy-done
  8.2 0.7 dynamic-slice_multiply_fusion
  8.9 0.3 multiply_reduce_fusion.3
  9.3 103.2 %all-reduce.4 = (f32[128]{0:T(128)S(1)}, f32[128]{0:T(128)S(1)}, f32[128]{0:T(128)S(1)}, f32[128]{0:T(128)S(1)}) all-reduce(f32[128]{0:T(128)S(1)} %get-tuple-element.8, f32[128]{0:T(128)S(1)} %get-tuple-element.7, f32[128]{0:T(128)S(1)} %get-tuple-element.6, ...), channel_id=1, replica_groups=mesh['row'=16,'col'=32] {'row','col'}, use_global_device_ids=true, to_apply=%region_10.0 | all-reduce | flops 512 | bytes 4096 | tf_op jit(solution)/shard_map/psum | solution.py:30
  112.5 1.0 multiply_convert_fusion.3
  113.5 0.0 all-gather.7.cloned.1.call-update
  113.5 0.0 all-gather.9.cloned.1.call-start
  113.5 0.7 all-gather.9.cloned.1.call-update
  114.2 0.0 all-gather.11.cloned.1.call-start
  114.3 0.7 all-gather.11.cloned.1.call-update
  115.0 0.0 all-gather.5.cloned.1.call-start
  115.0 0.5 all-gather.5.cloned.1.call-update
  115.5 0.0 all-reduce.8.cloned.1.call-start
  115.6 32.4 %all-gather.7.cloned.1.call-done = bf16[2,2048,128]{1,2,0:T(8,128)(2,1)} async-done(((bf16[2,128,128]{1,2,0:T(8,128)(2,1)}), bf16[2,2048,128]{1,2,0:T(8,128)(2,1)}) %all-gather.7.cloned.1.call-update) | async-done | bytes 1048592 | tf_op jit(solution)/shard_map/all_gather | solution.py:32
  148.0 4.0 fusion.1
  152.0 0.9 copy.10
  152.9 36.4 %all-gather.9.cloned.1.call-done = bf16[2,2048,128]{1,2,0:T(8,128)(2,1)} async-done(((bf16[2,128,128]{1,2,0:T(8,128)(2,1)}), bf16[2,2048,128]{1,2,0:T(8,128)(2,1)}) %all-gather.9.cloned.1.call-update) | async-done | bytes 1048592 | tf_op jit(solution)/shard_map/all_gather | solution.py:32
  189.3 4.0 fusion.2
  193.3 0.9 copy.11
  194.2 36.4 %all-gather.11.cloned.1.call-done = bf16[2,2048,128]{1,2,0:T(8,128)(2,1)} async-done(((bf16[2,128,128]{1,2,0:T(8,128)(2,1)}), bf16[2,2048,128]{1,2,0:T(8,128)(2,1)}) %all-gather.11.cloned.1.call-update) | async-done | bytes 1048592 | tf_op jit(solution)/shard_map/all_gather | solution.py:32
  230.6 4.0 fusion.3
  234.6 0.9 copy.12
  235.5 36.2 %all-gather.5.cloned.1.call-done = bf16[2,2048,128]{1,2,0:T(8,128)(2,1)} async-done(((bf16[2,128,128]{1,2,0:T(8,128)(2,1)}), bf16[2,2048,128]{1,2,0:T(8,128)(2,1)}) %all-gather.5.cloned.1.call-update) | async-done | bytes 1048592 | tf_op jit(solution)/shard_map/all_gather | solution.py:32
  271.8 4.0 fusion
  275.8 0.9 copy.9
  276.7 0.0 all-reduce.8.cloned.1.call-update
  276.7 1.3 dynamic-slice
  278.6 160.0 %all-reduce.8.cloned.1.call-done = (bf16[2,512,128]{2,0,1:T(2,128)(2,1)}, bf16[2,512,128]{2,0,1:T(2,128)(2,1)}, bf16[2,512,128]{2,0,1:T(2,128)(2,1)}, bf16[2,512,128]{2,0,1:T(2,128)(2,1)}) async-done(((bf16[2,512,128]{2,0,1:T(2,128)(2,1)}, bf16[2,512,128]{2,0,1:T(2,128)(2,1)}, bf16[2,512,128]{2,0,1:T(2,128)(2,1)}, bf16[2,512,128]{2,0,1:T(2,128)(2,1)}), (bf16[2,512,128]{2,0,1:T(2,128)(2,1)}, ...) | async-done | bytes 1048592
  438.7 0.7 constant_dynamic-slice_fusion.3
  439.4 0.7 constant_dynamic-slice_fusion.2
  440.1 0.7 constant_dynamic-slice_fusion.1
  440.8 0.7 constant_dynamic-slice_fusion
  441.5 0.6 pad_maximum_fusion
  (9 shorter events, 0.0 us)
Async XLA Ops:
  6.5 1.7 copy-start
  6.5 141.5 %all-gather.7.cloned.1.call-start = ((), (), s32[]{:S(2)}) async-start(), calls=%async_computation.1 | async-start | bytes 1114112 | tf_op jit(solution)/shard_map/all_gather | solution.py:32
  113.5 75.8 %all-gather.9.cloned.1.call-start = ((), (), s32[]{:S(2)}) async-start(), calls=%async_computation.2 | async-start | bytes 1114112 | tf_op jit(solution)/shard_map/all_gather | solution.py:32
  114.2 116.4 %all-gather.11.cloned.1.call-start = ((), (), s32[]{:S(2)}) async-start(), calls=%async_computation.3 | async-start | bytes 1114112 | tf_op jit(solution)/shard_map/all_gather | solution.py:32
  115.0 156.8 %all-gather.5.cloned.1.call-start = ((), (), s32[]{:S(2)}) async-start(), calls=%async_computation | async-start | bytes 1114112 | tf_op jit(solution)/shard_map/all_gather | solution.py:32
  115.5 323.1 %all-reduce.8.cloned.1.call-start = ((), (), s32[]{:S(2)}) async-start(), calls=%async_computation.4 | async-start | bytes 2097152
Sparse Core Ops, SparseCore 0:
  113.6 34.3 all-gather.6
  150.0 39.2 all-gather.8
  191.3 39.2 all-gather.10
  232.5 39.2 all-gather.4
  276.8 161.8 all-reduce.7
where the time goes:
time: 450 us; the launch traced here: 449 us
  waiting for transfers between devices  303 us (67%)
  blocking collectives  103 us (23%)
  matrix products  16.2 us (4%)
  between operations  13.9 us (3%)
  local copies, waits for them, and re-layouts  9.3 us (2%)
    unnamed x6, waiting for transfers between devices  162 us
    all_gather x4, waiting for transfers between devices, local(): panel_block = lax.all_gather(panel_block, 'row', axis=1, tiled=True)  141 us
    psum x1, blocking collectives, local(): lax.psum(squares, ('row', 'col'))  103 us
    dot_general x4, matrix products, local(): jnp.einsum('crh,chm->crm', child_vectors, panel_block, preferred_element_...  16.2 us
  transfers between devices with their start and end apart: 5, of which 5 were waited for; matrix products, arithmetic and copies ran while one was open for 4% of the time, Pallas kernels for 0%

commit v1 on v0

v1 whole, which is shorter than its diff:
```python
import jax
import jax.numpy as jnp
from jax import lax
from jax.experimental import pallas as pl
from jax.experimental.pallas import tpu as pltpu
from jax.sharding import PartitionSpec as P

NX = 4
NZ = 8
MESH = pl.DeviceIdType.MESH
STAGES = ((0, 0), (1, 0), (0, 1), (1, 1))
WIDTH = 256


def kernel(
    vectors_hbm,
    position_ref,
    fraction_ref,
    weight_ref,
    keep_ref,
    root_ref,
    offset_ref,
    out_ref,
    vectors,
    panel,
    poles,
    roots,
    squares,
    part,
    ring,
    sent,
    arrived,
    spread,
    landed,
    own_total,
    x_totals,
    z_own,
    z_totals,
    load_sem,
    x_send,
    x_recv,
    z_send,
    z_recv,
    tx_send,
    tx_recv,
    tz_send,
    tz_recv,
):
    col = lax.axis_index("col")
    z = col // NX
    x = col % NX

    def at(zz, xx):
        return {"col": zz * NX + xx}

    right = (x + 1) % NX
    left = (x + NX - 1) % NX
    across = (x + 2) % NX
    z_peers = [(z + d) % NZ for d in (4, 3, 5, 2, 6, 1, 7)]

    barrier = pltpu.get_barrier_semaphore()
    for xx in (right, left, across):
        pl.semaphore_signal(barrier, inc=1, device_id=at(z, xx), device_id_type=MESH)
    for zz in z_peers:
        pl.semaphore_signal(barrier, inc=1, device_id=at(zz, x), device_id_type=MESH)

    loads = []
    for child in range(2):
        copies = []
        for xx in range(NX):
            copy = pltpu.make_async_copy(
                vectors_hbm.at[child, :, xx], vectors.at[child, xx], load_sem.at[child, xx]
            )
            copy.start()
            copies.append(copy)
        loads.append(copies)

    half = position_ref.shape[1]
    for child in range(2):
        row = slice(child, child + 1)
        poles[child, 0] = jnp.broadcast_to(position_ref[row, :].astype(jnp.float32), (8, half))
        poles[child, 1] = jnp.broadcast_to(fraction_ref[row, :], (8, half))
        poles[child, 2] = jnp.broadcast_to(
            keep_ref[row, :].astype(jnp.float32) * weight_ref[row, :], (8, half)
        )
    for block in range(4):
        lanes = slice(block * 128, block * 128 + 128)
        roots[0, block * 16 : block * 16 + 16] = jnp.broadcast_to(
            root_ref[:, lanes].astype(jnp.float32), (128, 128)
        ).T.reshape(16, 8, 128)
        roots[1, block * 16 : block * 16 + 16] = jnp.broadcast_to(
            offset_ref[:, lanes], (128, 128)
        ).T.reshape(16, 8, 128)

    def make_panel(child, side):
        def body(step, carry):
            first = side * 32 + step * 4
            root_rows = roots[0, pl.ds(first, 4)]
            offset_rows = roots[1, pl.ds(first, 4)]
            total = jnp.zeros((4, 8, 128), jnp.float32)
            for block in range(half // 128):
                lanes = slice(block * 128, block * 128 + 128)
                spacing = (poles[child, 0, :, lanes][None] - root_rows) + (
                    poles[child, 1, :, lanes][None] - offset_rows
                )
                raw = poles[child, 2, :, lanes][None] / spacing
                total = total + raw * raw
                panel[child, pl.ds(pl.multiple_of(first * 8, 32), 32), lanes] = raw.reshape(
                    32, 128
                ).astype(jnp.bfloat16)
            if child == 0:
                squares[pl.ds(first, 4)] = total
            else:
                squares[pl.ds(first, 4)] = squares[pl.ds(first, 4)] + total
            return carry

        lax.fori_loop(0, 8, body, 0)

    def remote(src, dst, send, recv, target):
        return pltpu.make_async_remote_copy(
            src_ref=src, dst_ref=dst, send_sem=send, recv_sem=recv, device_id=target, device_id_type=MESH
        )

    upper, lower = pl.ds(0, 4), pl.ds(4, 4)
    x_copies = {}
    z_copies = {}

    def send_first(s):
        for d, (near, far, near_half, far_half) in enumerate(
            ((right, across, lower, upper), (left, across, upper, lower))
        ):
            x_copies[s, d, 0] = remote(
                part.at[s, far, far_half],
                ring.at[s, d],
                x_send.at[s, d, 0],
                x_recv.at[s, d, 0],
                at(z, near),
            )
            x_copies[s, d, 1] = remote(
                part.at[s, near, near_half],
                arrived.at[s, d, near_half],
                x_send.at[s, d, 1],
                x_recv.at[s, d, 1],
                at(z, near),
            )
            x_copies[s, d, 0].start()
            x_copies[s, d, 1].start()

    def send_second(s):
        for d, (near, half_rows) in enumerate(((right, upper), (left, lower))):
            x_copies[s, d, 0].wait_recv()
            sent[s, d] = (
                part[s, near, half_rows].astype(jnp.float32) + ring[s, d].astype(jnp.float32)
            ).astype(jnp.bfloat16)
            x_copies[s, d, 2] = remote(
                sent.at[s, d],
                arrived.at[s, d, half_rows],
                x_send.at[s, d, 2],
                x_recv.at[s, d, 2],
                at(z, near),
            )
            x_copies[s, d, 2].start()

    def send_third(s):
        for d in range(2):
            x_copies[s, d, 1].wait_recv()
            x_copies[s, d, 2].wait_recv()
        spread[s] = (
            part[s, x].astype(jnp.float32)
            + arrived[s, 0].astype(jnp.float32)
            + arrived[s, 1].astype(jnp.float32)
        ).astype(jnp.bfloat16)
        for n, zz in enumerate(z_peers):
            z_copies[s, n] = remote(
                spread.at[s, zz], landed.at[s, n], z_send.at[s, n], z_recv.at[s, n], at(zz, x)
            )
            z_copies[s, n].start()

    for s, (child, side) in enumerate(STAGES):
        make_panel(child, side)
        if side == 0:
            for copy in loads[child]:
                copy.wait()
        block = lax.dot_general(
            vectors[child].reshape(NX * NZ * 16, half),
            panel[child, side * WIDTH : side * WIDTH + WIDTH, :],
            (((1,), (1,)), ((), ())),
            preferred_element_type=jnp.float32,
        )
        part[s] = block.astype(jnp.bfloat16).reshape(NX, NZ, 16, WIDTH)
        if s == 0:
            pl.semaphore_wait(barrier, NX - 1 + NZ - 1)
        send_first(s)
        if s >= 1:
            send_second(s - 1)
        if s >= 2:
            send_third(s - 2)

    for block in range(4):
        own_total[:, block * 128 : block * 128 + 128] = jnp.broadcast_to(
            jnp.sum(squares[block * 16 : block * 16 + 16].reshape(128, 128).T, axis=0, keepdims=True),
            (8, 128),
        )
    tx_copies = []
    for n, xx in enumerate((across, right, left)):
        copy = remote(own_total, x_totals.at[n], tx_send.at[n], tx_recv.at[n], at(z, xx))
        copy.start()
        tx_copies.append(copy)

    last = len(STAGES) - 1
    send_second(last)
    send_third(last - 1)
    for copy in tx_copies:
        copy.wait_recv()
    z_own[...] = own_total[...] + x_totals[0] + x_totals[1] + x_totals[2]
    tz_copies = []
    for n, zz in enumerate(z_peers):
        copy = remote(z_own, z_totals.at[n], tz_send.at[n], tz_recv.at[n], at(zz, x))
        copy.start()
        tz_copies.append(copy)
    send_third(last)

    total = z_own[...]
    for n, copy in enumerate(tz_copies):
        copy.wait_recv()
        total = total + z_totals[n]
    scale = lax.rsqrt(total)
    for s, (child, side) in enumerate(STAGES):
        result = spread[s, z].astype(jnp.float32)
        for n in range(len(z_peers)):
            z_copies[s, n].wait_recv()
            result = result + landed[s, n].astype(jnp.float32)
        lanes = slice(side * WIDTH, side * WIDTH + WIDTH)
        out_ref[child, :, lanes] = (result * scale[0:1, lanes]).astype(jnp.bfloat16)

    for copy in list(x_copies.values()) + list(z_copies.values()) + tx_copies + tz_copies:
        copy.wait_send()


def local(child_vectors, merge_position, pole_frac, weights, retained, root_index, root_offset):
    children, rows, half = child_vectors.shape
    cols = root_index.shape[0]
    stages = len(STAGES)
    bf16, f32 = jnp.bfloat16, jnp.float32
    dma = pltpu.SemaphoreType.DMA
    vmem = pl.BlockSpec(memory_space=pltpu.VMEM)
    return pl.pallas_call(
        kernel,
        out_shape=jax.ShapeDtypeStruct((children, 16, cols), bf16),
        in_specs=[pl.BlockSpec(memory_space=pl.ANY)] + [vmem] * 6,
        out_specs=vmem,
        scratch_shapes=[
            pltpu.VMEM((children, NX, NZ, 16, half), bf16),
            pltpu.VMEM((children, cols, half), bf16),
            pltpu.VMEM((children, 3, 8, half), f32),
            pltpu.VMEM((2, cols // 8, 8, 128), f32),
            pltpu.VMEM((cols // 8, 8, 128), f32),
            pltpu.VMEM((stages, NX, NZ, 16, WIDTH), bf16),
            pltpu.VMEM((stages, 2, NZ // 2, 16, WIDTH), bf16),
            pltpu.VMEM((stages, 2, NZ // 2, 16, WIDTH), bf16),
            pltpu.VMEM((stages, 2, NZ, 16, WIDTH), bf16),
            pltpu.VMEM((stages, NZ, 16, WIDTH), bf16),
            pltpu.VMEM((stages, NZ - 1, 16, WIDTH), bf16),
            pltpu.VMEM((8, cols), f32),
            pltpu.VMEM((NX - 1, 8, cols), f32),
            pltpu.VMEM((8, cols), f32),
            pltpu.VMEM((NZ - 1, 8, cols), f32),
            dma((children, NX)),
            dma((stages, 2, 3)),
            dma((stages, 2, 3)),
            dma((stages, NZ - 1)),
            dma((stages, NZ - 1)),
            dma((NX - 1,)),
            dma((NX - 1,)),
            dma((NZ - 1,)),
            dma((NZ - 1,)),
        ],
        compiler_params=pltpu.CompilerParams(collective_id=0, has_side_effects=True),
        name="panel_product",
    )(
        child_vectors.reshape(children, NZ, NX, 16, half),
        merge_position,
        pole_frac,
        weights,
        retained,
        root_index.reshape(1, cols),
        root_offset.reshape(1, cols),
    )


def solution(mesh):
    return jax.shard_map(
        local,
        mesh=mesh,
        in_specs=(
            P(None, "row", "col"),
            P(None, "col"),
            P(None, "col"),
            P(None, "col"),
            P(None, "col"),
            P(),
            P(),
        ),
        out_specs=P(None, ("row", "col"), None),
        check_vma=False,
    )
```

time: 450 us -> 36.3 us (0.08)
  waiting for transfers between devices: 303 us -> 0 us
  blocking collectives: 103 us -> 0 us
  Pallas kernels: 0 us -> 34.7 us
  matrix products: 16.2 us -> 0 us
  between operations: 13.9 us -> 0.01 us
  local copies, waits for them, and re-layouts: 9.3 us -> 1.38 us
    unnamed x6 -> x0, waiting for transfers between devices: 162 us -> none
    all_gather x4 -> x0, waiting for transfers between devices: 141 us -> none  [local(): panel_block = lax.all_gather(panel_block, 'row', axis=1, tiled=True)]
    psum x1 -> x0, blocking collectives: 103 us -> none  [local(): lax.psum(squares, ('row', 'col'))]
    pallas_call x0 -> x1, Pallas kernels: none -> 34.7 us  [local(): pl.pallas_call(kernel, out_shape=jax.ShapeDtypeStruct((children, 16, cols...]
    dot_general x4 -> x0, matrix products: 16.2 us -> none  [local(): jnp.einsum('crh,chm->crm', child_vectors, panel_block, preferred_element_...]
  transfers between devices with their start and end apart: 5 -> 0, of which waited for: 5 -> 0; matrix products, arithmetic and copies ran while one was open for 4% -> 0% of each run, Pallas kernels for 0% -> 0%
where the time goes in v1:
time: 36.3 us; the launch traced here: 36.1 us
  Pallas kernels  34.7 us (96%)
  local copies, waits for them, and re-layouts  1.38 us (4%)
    pallas_call x1, Pallas kernels, local(): pl.pallas_call(kernel, out_shape=jax.ShapeDtypeStruct((children, 16, cols...  34.7 us
    unnamed x1, local copies, waits for them, and re-layouts  1.38 us

profile of v1, /device:TPU:56, one launch (start us, length us, event | category | flops | bytes accessed | tf_op | source)
XLA Modules:
  0.0 36.1 jit_solution(3707370480735307484)
XLA Ops:
  0.0 34.7 %panel_product.1 = bf16[2,16,512]{2,1,0:T(8,128)(2,1)} custom-call(bf16[2,8,4,16,2048]{4,3,2,1,0:T(8,128)(2,1)} %bitcast.3, s32[2,2048]{1,0:T(2,128)} %position_ref.1, f32[2,2048]{1,0:T(2,128)} %fraction_ref.1, f32[2,2048]{1,0:T(2,128)} %weight_ref.1, s32[2,2048]{1,0:T(2,128)} %keep_ref.1, s32[1,512]{1,0:T(1,128)} %bitcast.4, f32[1,512]{1,0:T(1,128)} %bitcast.5), custom_call_target="tpu_custom_call" | custom-call | tf_op jit(solution)/shard_map/panel_product/pallas_call | solution.py:247
  34.7 1.4 %copy.9 = bf16[2,16,512]{2,1,0:T(8,128)(2,1)} copy(bf16[2,16,512]{2,1,0:T(8,128)(2,1)} %panel_product.1) | data formatting | bytes 65536

commit v2 on v1

v2 whole, which is shorter than its diff:
```python
import jax
import jax.numpy as jnp
from jax import lax
from jax.experimental import pallas as pl
from jax.experimental.pallas import tpu as pltpu
from jax.sharding import PartitionSpec as P

NX = 4
NZ = 8
MESH = pl.DeviceIdType.MESH
OWNERS = NZ // 2
WIDTH = 256


def kernel(
    vectors_hbm,
    position_hbm,
    fraction_hbm,
    weight_hbm,
    keep_hbm,
    root_hbm,
    offset_hbm,
    out_ref,
    position_ref,
    fraction_ref,
    weight_ref,
    keep_ref,
    root_ref,
    offset_ref,
    vectors,
    panel,
    poles,
    roots,
    squares,
    part,
    arrived,
    spread,
    landed,
    own_total,
    x_totals,
    z_own,
    z_totals,
    small_sem,
    load_sem,
    x_send,
    x_recv,
    z_send,
    z_recv,
    tx_send,
    tx_recv,
    tz_send,
    tz_recv,
):
    small = []
    for n, (source, target) in enumerate(
        (
            (root_hbm, root_ref),
            (offset_hbm, offset_ref),
            (position_hbm, position_ref),
            (fraction_hbm, fraction_ref),
            (weight_hbm, weight_ref),
            (keep_hbm, keep_ref),
        )
    ):
        copy = pltpu.make_async_copy(source, target, small_sem.at[n])
        copy.start()
        small.append(copy)

    col = lax.axis_index("col")
    z = col // NX
    x = col % NX

    def at(zz, xx):
        return {"col": zz * NX + xx}

    x_peers = [(x + d) % NX for d in (2, 1, 3)]
    z_peers = [(z + d) % NZ for d in (4, 3, 5, 2, 6, 1, 7)]

    barrier = pltpu.get_barrier_semaphore()
    for xx in x_peers:
        pl.semaphore_signal(barrier, inc=1, device_id=at(z, xx), device_id_type=MESH)
    for zz in z_peers:
        pl.semaphore_signal(barrier, inc=1, device_id=at(zz, x), device_id_type=MESH)

    loads = {}
    for child in range(2):
        for group in range(2):
            owners = pl.ds(group * OWNERS, OWNERS)
            loads[group, child] = []
            for xx in range(NX):
                copy = pltpu.make_async_copy(
                    vectors_hbm.at[child, owners, xx],
                    vectors.at[group, child, xx],
                    load_sem.at[group, child, xx],
                )
                copy.start()
                loads[group, child].append(copy)

    for copy in small:
        copy.wait()

    half = position_ref.shape[1]
    for child in range(2):
        row = slice(child, child + 1)
        poles[child, 0] = jnp.broadcast_to(position_ref[row, :].astype(jnp.float32), (8, half))
        poles[child, 1] = jnp.broadcast_to(fraction_ref[row, :], (8, half))
        poles[child, 2] = jnp.broadcast_to(
            keep_ref[row, :].astype(jnp.float32) * weight_ref[row, :], (8, half)
        )
    for block in range(4):
        lanes = slice(block * 128, block * 128 + 128)
        roots[0, block * 16 : block * 16 + 16] = jnp.broadcast_to(
            root_ref[:, lanes].astype(jnp.float32), (128, 128)
        ).T.reshape(16, 8, 128)
        roots[1, block * 16 : block * 16 + 16] = jnp.broadcast_to(
            offset_ref[:, lanes], (128, 128)
        ).T.reshape(16, 8, 128)

    def make_panel(child, side):
        def body(step, carry):
            first = side * 32 + step * 4
            root_rows = roots[0, pl.ds(first, 4)]
            offset_rows = roots[1, pl.ds(first, 4)]
            total = jnp.zeros((4, 8, 128), jnp.float32)
            for block in range(half // 128):
                lanes = slice(block * 128, block * 128 + 128)
                spacing = (poles[child, 0, :, lanes][None] - root_rows) + (
                    poles[child, 1, :, lanes][None] - offset_rows
                )
                raw = poles[child, 2, :, lanes][None] / spacing
                total = total + raw * raw
                panel[child, pl.ds(pl.multiple_of(first * 8, 32), 32), lanes] = raw.reshape(
                    32, 128
                ).astype(jnp.bfloat16)
            if child == 0:
                squares[pl.ds(first, 4)] = total
            else:
                squares[pl.ds(first, 4)] = squares[pl.ds(first, 4)] + total
            return carry

        lax.fori_loop(0, 8, body, 0)

    def remote(src, dst, send, recv, target):
        return pltpu.make_async_remote_copy(
            src_ref=src, dst_ref=dst, send_sem=send, recv_sem=recv, device_id=target, device_id_type=MESH
        )

    x_copies = {}
    z_copies = {}

    def multiply(group, child, first, count):
        columns = slice(first * WIDTH, (first + count) * WIDTH)
        block = lax.dot_general(
            vectors[group, child].reshape(NX * OWNERS * 16, half),
            panel[child, columns],
            (((1,), (1,)), ((), ())),
            preferred_element_type=jnp.float32,
        ).astype(jnp.bfloat16)
        for n in range(count):
            part[group, child, first + n] = block[:, n * WIDTH : n * WIDTH + WIDTH].reshape(NX, OWNERS, 16, WIDTH)

    def send_x(group, child, side):
        unit = (group, child, side)
        for n, xx in enumerate(x_peers):
            copy = remote(
                part.at[group, child, side, xx],
                arrived.at[group, child, side, n],
                x_send.at[group, child, side, n],
                x_recv.at[group, child, side, n],
                at(z, xx),
            )
            copy.start()
            x_copies[unit + (n,)] = copy

    def z_copy(child, side, n):
        return remote(
            spread.at[child, side, z_peers[n]],
            landed.at[child, side, n],
            z_send.at[child, side, n],
            z_recv.at[child, side, n],
            at(z_peers[n], x),
        )

    def send_z(group, child, side):
        total = part[group, child, side, x].astype(jnp.float32)
        for n in range(NX - 1):
            x_copies[group, child, side, n].wait_recv()
            total = total + arrived[group, child, side, n].astype(jnp.float32)
        spread[child, side, group * OWNERS : (group + 1) * OWNERS] = total.astype(jnp.bfloat16)
        for n, zz in enumerate(z_peers):

            @pl.when(zz // OWNERS == group)
            def _(n=n):
                z_copy(child, side, n).start()

    tx_copies = []
    for child in range(2):
        for side in range(2):
            make_panel(child, side)
            if child == 1:
                for block in range(2 * side, 2 * side + 2):
                    own_total[block : block + 1] = jnp.sum(
                        squares[block * 16 : block * 16 + 16].reshape(128, 128).T, axis=0, keepdims=True
                    )
            if side == 0:
                for copy in loads[0, child]:
                    copy.wait()
            multiply(0, child, side, 1)
            if (child, side) == (0, 0):
                pl.semaphore_wait(barrier, NX - 1 + NZ - 1)
            if (child, side) == (1, 1):
                for n, xx in enumerate(x_peers):
                    copy = remote(own_total, x_totals.at[n], tx_send.at[n], tx_recv.at[n], at(z, xx))
                    copy.start()
                    tx_copies.append(copy)
            send_x(0, child, side)

    for child in range(2):
        for copy in loads[1, child]:
            copy.wait()
        multiply(1, child, 0, 2)
        send_x(1, child, 0)
        send_x(1, child, 1)
        send_z(0, 0, child)

    send_z(0, 1, 0)
    for copy in tx_copies:
        copy.wait_recv()
    z_own[...] = own_total[...] + x_totals[0] + x_totals[1] + x_totals[2]
    tz_copies = []
    for n, zz in enumerate(z_peers):
        copy = remote(z_own, z_totals.at[n], tz_send.at[n], tz_recv.at[n], at(zz, x))
        copy.start()
        tz_copies.append(copy)
    send_z(0, 1, 1)
    for child in range(2):
        for side in range(2):
            send_z(1, child, side)

    total = z_own[...]
    for n, copy in enumerate(tz_copies):
        copy.wait_recv()
        total = total + z_totals[n]
    scale = lax.rsqrt(total)
    for child in range(2):
        for side in range(2):
            result = spread[child, side, z].astype(jnp.float32)
            for n in range(NZ - 1):
                z_copy(child, side, n).wait_recv()
                result = result + landed[child, side, n].astype(jnp.float32)
            for block in range(2 * side, 2 * side + 2):
                lanes = slice(block * 128 - side * WIDTH, block * 128 - side * WIDTH + 128)
                out_ref[child, :, block * 128 : block * 128 + 128] = (
                    result[:, lanes] * scale[block : block + 1]
                ).astype(jnp.bfloat16)

    for child in range(2):
        for side in range(2):
            for n in range(NZ - 1):
                z_copy(child, side, n).wait_send()
    for copy in list(x_copies.values()) + tx_copies + tz_copies:
        copy.wait_send()


def local(child_vectors, merge_position, pole_frac, weights, retained, root_index, root_offset):
    children, rows, half = child_vectors.shape
    cols = root_index.shape[0]
    bf16, f32 = jnp.bfloat16, jnp.float32
    dma = pltpu.SemaphoreType.DMA
    sides = cols // WIDTH
    return pl.pallas_call(
        kernel,
        out_shape=jax.ShapeDtypeStruct((children, 16, cols), bf16),
        in_specs=[pl.BlockSpec(memory_space=pltpu.HBM)] * 7,
        out_specs=pl.BlockSpec(memory_space=pltpu.VMEM),
        scratch_shapes=[
            pltpu.VMEM((children, half), jnp.int32),
            pltpu.VMEM((children, half), f32),
            pltpu.VMEM((children, half), f32),
            pltpu.VMEM((children, half), jnp.int32),
            pltpu.VMEM((1, cols), jnp.int32),
            pltpu.VMEM((1, cols), f32),
            pltpu.VMEM((2, children, NX, OWNERS, 16, half), bf16),
            pltpu.VMEM((children, cols, half), bf16),
            pltpu.VMEM((children, 3, 8, half), f32),
            pltpu.VMEM((2, cols // 8, 8, 128), f32),
            pltpu.VMEM((cols // 8, 8, 128), f32),
            pltpu.VMEM((2, children, sides, NX, OWNERS, 16, WIDTH), bf16),
            pltpu.VMEM((2, children, sides, NX - 1, OWNERS, 16, WIDTH), bf16),
            pltpu.VMEM((children, sides, NZ, 16, WIDTH), bf16),
            pltpu.VMEM((children, sides, NZ - 1, 16, WIDTH), bf16),
            pltpu.VMEM((cols // 128, 128), f32),
            pltpu.VMEM((NX - 1, cols // 128, 128), f32),
            pltpu.VMEM((cols // 128, 128), f32),
            pltpu.VMEM((NZ - 1, cols // 128, 128), f32),
            dma((6,)),
            dma((2, children, NX)),
            dma((2, children, sides, NX - 1)),
            dma((2, children, sides, NX - 1)),
            dma((children, sides, NZ - 1)),
            dma((children, sides, NZ - 1)),
            dma((NX - 1,)),
            dma((NX - 1,)),
            dma((NZ - 1,)),
            dma((NZ - 1,)),
        ],
        compiler_params=pltpu.CompilerParams(
            collective_id=0, has_side_effects=True, vmem_limit_bytes=24 * 2**20
        ),
        name="panel_product",
    )(
        *(
            pltpu.with_memory_space_constraint(value, pltpu.HBM)
            for value in (
                child_vectors.reshape(children, NZ, NX, 16, half),
                merge_position,
                pole_frac,
                weights,
                retained,
                root_index.reshape(1, cols),
                root_offset.reshape(1, cols),
            )
        )
    )


def solution(mesh):
    return jax.shard_map(
        local,
        mesh=mesh,
        in_specs=(
            P(None, "row", "col"),
            P(None, "col"),
            P(None, "col"),
            P(None, "col"),
            P(None, "col"),
            P(),
            P(),
        ),
        out_specs=P(None, ("row", "col"), None),
        check_vma=False,
    )
```

time: 36.3 us -> 28.8 us (0.79)
  Pallas kernels: 34.7 us -> 28 us
  local copies, waits for them, and re-layouts: 1.38 us -> 0.62 us
    pallas_call x1, Pallas kernels: 34.7 us -> 28 us  [local(): pl.pallas_call(kernel, out_shape=jax.ShapeDtypeStruct((children, 16, cols...]
    unnamed x1, local copies, waits for them, and re-layouts: 1.38 us -> 0.62 us
where the time goes in v2:
time: 28.8 us; the launch traced here: 28.6 us
  Pallas kernels  28 us (97%)
  local copies, waits for them, and re-layouts  0.62 us (2%)
    pallas_call x1, Pallas kernels, local(): pl.pallas_call(kernel, out_shape=jax.ShapeDtypeStruct((children, 16, cols...  28 us
    unnamed x1, local copies, waits for them, and re-layouts  0.62 us

profile of v2, /device:TPU:56, one launch (start us, length us, event | category | flops | bytes accessed | tf_op | source)
XLA Modules:
  0.0 28.6 jit_solution(2234448576796024755)
XLA Ops:
  0.0 28.0 %panel_product.1 = bf16[2,16,512]{2,1,0:T(8,128)(2,1)S(1)} custom-call(bf16[2,8,4,16,2048]{4,3,2,1,0:T(8,128)(2,1)} %bitcast.3, s32[2,2048]{1,0:T(2,128)} %position_hbm.1, f32[2,2048]{1,0:T(2,128)} %fraction_hbm.1, f32[2,2048]{1,0:T(2,128)} %weight_hbm.1, s32[2,2048]{1,0:T(2,128)} %keep_hbm.1, s32[1,512]{1,0:T(1,128)} %bitcast.4, f32[1,512]{1,0:T(1,128)} %bitcast.5), custom_call_target="tpu_custom_call" | custom-call | tf_op jit(solution)/shard_map/panel_product/pallas_call | solution.py:271
  28.0 0.6 %copy.9 = bf16[2,16,512]{2,1,0:T(8,128)(2,1)} copy(bf16[2,16,512]{2,1,0:T(8,128)(2,1)S(1)} %panel_product.1) | data formatting | bytes 65536

commit v3 on v2

--- a/solution.py
+++ b/solution.py
@@ -40,6 +40,9 @@
     x_totals,
     z_own,
     z_totals,
+    scale,
+    x_ready,
+    z_ready,
     small_sem,
     load_sem,
     x_send,
@@ -76,26 +79,47 @@
     x_peers = [(x + d) % NX for d in (2, 1, 3)]
     z_peers = [(z + d) % NZ for d in (4, 3, 5, 2, 6, 1, 7)]
 
+    hub_x = 3 - (z // 6 - z // 7)
+    hub_z = 7 - x // 3
     barrier = pltpu.get_barrier_semaphore()
-    for xx in x_peers:
-        pl.semaphore_signal(barrier, inc=1, device_id=at(z, xx), device_id_type=MESH)
-    for zz in z_peers:
-        pl.semaphore_signal(barrier, inc=1, device_id=at(zz, x), device_id_type=MESH)
-
-    loads = {}
-    for child in range(2):
-        for group in range(2):
-            owners = pl.ds(group * OWNERS, OWNERS)
-            loads[group, child] = []
-            for xx in range(NX):
-                copy = pltpu.make_async_copy(
-                    vectors_hbm.at[child, owners, xx],
-                    vectors.at[group, child, xx],
-                    load_sem.at[group, child, xx],
-                )
-                copy.start()
-                loads[group, child].append(copy)
-
+
+    @pl.when(x != hub_x)
+    def _():
+        pl.semaphore_signal(barrier, inc=1, device_id=at(z, hub_x), device_id_type=MESH)
+
+    @pl.when(z != hub_z)
+    def _():
+        pl.semaphore_signal(barrier, inc=1, device_id=at(hub_z, x), device_id_type=MESH)
+
+    def answer():
+        @pl.when(x == hub_x)
+        def _():
+            pl.semaphore_wait(barrier, NX - 1)
+            for xx in x_peers:
+                pl.semaphore_signal(x_ready, inc=1, device_id=at(z, xx), device_id_type=MESH)
+
+        @pl.when(z == hub_z)
+        def _():
+            pl.semaphore_wait(barrier, NZ - 1)
+            for zz in z_peers:
+                pl.semaphore_signal(z_ready, inc=1, device_id=at(zz, x), device_id_type=MESH)
+
+    def load(group, child, xx):
+        return pltpu.make_async_copy(
+            vectors_hbm.at[child, pl.ds(group * OWNERS, OWNERS), xx],
+            vectors.at[group, child, xx],
+            load_sem.at[group, child, xx],
+        )
+
+    def wait_loads(group, child):
+        for xx in range(NX):
+            load(group, child, xx).wait()
+
+    def start_loads(group, child):
+        for xx in range(NX):
+            load(group, child, xx).start()
+
+    start_loads(0, 0)
     for copy in small:
         copy.wait()
 
@@ -116,7 +140,9 @@
             offset_ref[:, lanes], (128, 128)
         ).T.reshape(16, 8, 128)
 
-    def make_panel(child, side):
+    squares[...] = jnp.zeros_like(squares)
+
+    def make_panel(child, side, start, stop):
         def body(step, carry):
             first = side * 32 + step * 4
             root_rows = roots[0, pl.ds(first, 4)]
@@ -132,45 +158,36 @@
                 panel[child, pl.ds(pl.multiple_of(first * 8, 32), 32), lanes] = raw.reshape(
                     32, 128
                 ).astype(jnp.bfloat16)
-            if child == 0:
-                squares[pl.ds(first, 4)] = total
-            else:
-                squares[pl.ds(first, 4)] = squares[pl.ds(first, 4)] + total
+            squares[pl.ds(first, 4)] = squares[pl.ds(first, 4)] + total
             return carry
 
-        lax.fori_loop(0, 8, body, 0)
+        lax.fori_loop(start, stop, body, 0)
 
     def remote(src, dst, send, recv, target):
         return pltpu.make_async_remote_copy(
             src_ref=src, dst_ref=dst, send_sem=send, recv_sem=recv, device_id=target, device_id_type=MESH
         )
 
-    x_copies = {}
-    z_copies = {}
-
-    def multiply(group, child, first, count):
-        columns = slice(first * WIDTH, (first + count) * WIDTH)
-        block = lax.dot_general(
+    def product(group, child, columns):
+        return lax.dot_general(
             vectors[group, child].reshape(NX * OWNERS * 16, half),
             panel[child, columns],
             (((1,), (1,)), ((), ())),
             preferred_element_type=jnp.float32,
         ).astype(jnp.bfloat16)
-        for n in range(count):
-            part[group, child, first + n] = block[:, n * WIDTH : n * WIDTH + WIDTH].reshape(NX, OWNERS, 16, WIDTH)
+
+    def x_copy(group, child, side, n):
+        return remote(
+            part.at[group, child, side, x_peers[n]],
+            arrived.at[group, child, side, n],
+            x_send.at[group, child, side, n],
+            x_recv.at[group, child, side, n],
+            at(z, x_peers[n]),
+        )
 
     def send_x(group, child, side):
-        unit = (group, child, side)
-        for n, xx in enumerate(x_peers):
-            copy = remote(
-                part.at[group, child, side, xx],
-                arrived.at[group, child, side, n],
-                x_send.at[group, child, side, n],
-                x_recv.at[group, child, side, n],
-                at(z, xx),
-            )
-            copy.start()
-            x_copies[unit + (n,)] = copy
+        for n in range(NX - 1):
+            x_copy(group, child, side, n).start()
 
     def z_copy(child, side, n):
         return remote(
@@ -184,82 +201,124 @@
     def send_z(group, child, side):
         total = part[group, child, side, x].astype(jnp.float32)
         for n in range(NX - 1):
-            x_copies[group, child, side, n].wait_recv()
+            x_copy(group, child, side, n).wait_recv()
             total = total + arrived[group, child, side, n].astype(jnp.float32)
-        spread[child, side, group * OWNERS : (group + 1) * OWNERS] = total.astype(jnp.bfloat16)
+        spread[child, side, pl.ds(group * OWNERS, OWNERS)] = total.astype(jnp.bfloat16)
         for n, zz in enumerate(z_peers):
 
             @pl.when(zz // OWNERS == group)
             def _(n=n):
                 z_copy(child, side, n).start()
 
-    tx_copies = []
-    for child in range(2):
+    def tx_copy(n):
+        return remote(own_total, x_totals.at[n], tx_send.at[n], tx_recv.at[n], at(z, x_peers[n]))
+
+    def tz_copy(n):
+        return remote(z_own, z_totals.at[n], tz_send.at[n], tz_recv.at[n], at(z_peers[n], x))
+
+    def loop(count):
+        def run(body):
+            lax.fori_loop(0, count, lambda step, carry: (body(step), carry)[1], 0)
+
+        return run
+
+    @loop(4)
+    def _(unit):
+        child, side = unit // 2, unit % 2
+        make_panel(child, side, 0, 4)
+        pl.when(unit == 0)(answer)
+        make_panel(child, side, 4, 8)
+
+        @pl.when(side == 0)
+        def _():
+            wait_loads(0, child)
+
+        @pl.when(unit == 0)
+        def _():
+            start_loads(0, 1)
+            start_loads(1, 0)
+            start_loads(1, 1)
+
+        columns = pl.ds(pl.multiple_of(side * WIDTH, WIDTH), WIDTH)
+        part[0, child, side] = product(0, child, columns).reshape(NX, OWNERS, 16, WIDTH)
+
+        @pl.when(jnp.logical_and(unit == 0, x != hub_x))
+        def _():
+            pl.semaphore_wait(x_ready, 1)
+
+        @pl.when(unit == 3)
+        def _():
+            for block in range(4):
+                own_total[block : block + 1] = jnp.sum(
+                    squares[block * 16 : block * 16 + 16].reshape(128, 128).T, axis=0, keepdims=True
+                )
+            for n in range(NX - 1):
+                tx_copy(n).start()
+
+        send_x(0, child, side)
+
+    @loop(2)
+    def _(child):
+        wait_loads(1, child)
+        block = product(1, child, slice(None))
         for side in range(2):
-            make_panel(child, side)
-            if child == 1:
-                for block in range(2 * side, 2 * side + 2):
-                    own_total[block : block + 1] = jnp.sum(
-                        squares[block * 16 : block * 16 + 16].reshape(128, 128).T, axis=0, keepdims=True
-                    )
-            if side == 0:
-                for copy in loads[0, child]:
-                    copy.wait()
-            multiply(0, child, side, 1)
-            if (child, side) == (0, 0):
-                pl.semaphore_wait(barrier, NX - 1 + NZ - 1)
-            if (child, side) == (1, 1):
-                for n, xx in enumerate(x_peers):
-                    copy = remote(own_total, x_totals.at[n], tx_send.at[n], tx_recv.at[n], at(z, xx))
-                    copy.start()
-                    tx_copies.append(copy)
-            send_x(0, child, side)
-
-    for child in range(2):
-        for copy in loads[1, child]:
-            copy.wait()
-        multiply(1, child, 0, 2)
-        send_x(1, child, 0)
-        send_x(1, child, 1)
+            part[1, child, side] = block[:, side * WIDTH : side * WIDTH + WIDTH].reshape(NX, OWNERS, 16, WIDTH)
+        for side in range(2):
+            send_x(1, child, side)
+
+        @pl.when(jnp.logical_and(child == 0, z != hub_z))
+        def _():
+            pl.semaphore_wait(z_ready, 1)
+
         send_z(0, 0, child)
 
-    send_z(0, 1, 0)
-    for copy in tx_copies:
-        copy.wait_recv()
-    z_own[...] = own_total[...] + x_totals[0] + x_totals[1] + x_totals[2]
-    tz_copies = []
-    for n, zz in enumerate(z_peers):
-        copy = remote(z_own, z_totals.at[n], tz_send.at[n], tz_recv.at[n], at(zz, x))
-        copy.start()
-        tz_copies.append(copy)
-    send_z(0, 1, 1)
-    for child in range(2):
-        for side in range(2):
-            send_z(1, child, side)
+    @loop(6)
+    def _(step):
+        unit = step + 2
+        group, child, side = unit // 4, unit // 2 % 2, unit % 2
+
+        @pl.when(step == 1)
+        def _():
+            for n in range(NX - 1):
+                tx_copy(n).wait_recv()
+            z_own[...] = own_total[...] + x_totals[0] + x_totals[1] + x_totals[2]
+            for n in range(NZ - 1):
+                tz_copy(n).start()
+
+        send_z(group, child, side)
 
     total = z_own[...]
-    for n, copy in enumerate(tz_copies):
-        copy.wait_recv()
+    for n in range(NZ - 1):
+        tz_copy(n).wait_recv()
         total = total + z_totals[n]
-    scale = lax.rsqrt(total)
-    for child in range(2):
-        for side in range(2):
-            result = spread[child, side, z].astype(jnp.float32)
-            for n in range(NZ - 1):
-                z_copy(child, side, n).wait_recv()
-                result = result + landed[child, side, n].astype(jnp.float32)
-            for block in range(2 * side, 2 * side + 2):
-                lanes = slice(block * 128 - side * WIDTH, block * 128 - side * WIDTH + 128)
-                out_ref[child, :, block * 128 : block * 128 + 128] = (
-                    result[:, lanes] * scale[block : block + 1]
-                ).astype(jnp.bfloat16)
-
-    for child in range(2):
-        for side in range(2):
-            for n in range(NZ - 1):
-                z_copy(child, side, n).wait_send()
-    for copy in list(x_copies.values()) + tx_copies + tz_copies:
-        copy.wait_send()
+    scale[...] = lax.rsqrt(total)
+
+    @loop(4)
+    def _(unit):
+        child, side = unit // 2, unit % 2
+        result = spread[child, side, z].astype(jnp.float32)
+        for n in range(NZ - 1):
+            z_copy(child, side, n).wait_recv()
+            result = result + landed[child, side, n].astype(jnp.float32)
+        for block in range(2):
+            first = pl.multiple_of(side * WIDTH + block * 128, 128)
+            out_ref[child, :, pl.ds(first, 128)] = (
+                result[:, block * 128 : block * 128 + 128] * scale[pl.ds(side * 2 + block, 1)]
+            ).astype(jnp.bfloat16)
+
+    @loop(4)
+    def _(unit):
+        child, side = unit // 2, unit % 2
+        for n in range(NX - 1):
+            x_copy(0, child, side, n).wait_send()
+            x_copy(1, child, side, n).wait_send()
+        for n in range(NZ - 1):
+            z_copy(child, side, n).wait_send()
+
+    for n in range(NX - 1):
+        tx_copy(n).wait_send()
+    for n in range(NZ - 1):
+        tz_copy(n).wait_send()
 
 
 def local(child_vectors, merge_position, pole_frac, weights, retained, root_index, root_offset):
@@ -293,6 +352,9 @@
             pltpu.VMEM((NX - 1, cols // 128, 128), f32),
             pltpu.VMEM((cols // 128, 128), f32),
             pltpu.VMEM((NZ - 1, cols // 128, 128), f32),
+            pltpu.VMEM((cols // 128, 128), f32),
+            pltpu.SemaphoreType.REGULAR,
+            pltpu.SemaphoreType.REGULAR,
             dma((6,)),
             dma((2, children, NX)),
             dma((2, children, sides, NX - 1)),

time: 28.8 us -> 27.7 us (0.962)
  the two profiles are of different devices: /device:TPU:56 before, /device:TPU:1 now
where the time goes in v3:
time: 27.7 us; the launch traced here: 27.6 us
  Pallas kernels  27 us (97%)
  local copies, waits for them, and re-layouts  0.62 us (2%)
    pallas_call x1, Pallas kernels, local(): pl.pallas_call(kernel, out_shape=jax.ShapeDtypeStruct((children, 16, cols...  27 us
    unnamed x1, local copies, waits for them, and re-layouts  0.62 us

profile of v3, /device:TPU:1, one launch (start us, length us, event | category | flops | bytes accessed | tf_op | source)
XLA Modules:
  0.0 27.6 jit_solution(1607109508765116272)
XLA Ops:
  0.0 27.0 %panel_product.1 = bf16[2,16,512]{2,1,0:T(8,128)(2,1)S(1)} custom-call(bf16[2,8,4,16,2048]{4,3,2,1,0:T(8,128)(2,1)} %bitcast.3, s32[2,2048]{1,0:T(2,128)} %position_hbm.1, f32[2,2048]{1,0:T(2,128)} %fraction_hbm.1, f32[2,2048]{1,0:T(2,128)} %weight_hbm.1, s32[2,2048]{1,0:T(2,128)} %keep_hbm.1, s32[1,512]{1,0:T(1,128)} %bitcast.4, f32[1,512]{1,0:T(1,128)} %bitcast.5), custom_call_target="tpu_custom_call" | custom-call | tf_op jit(solution)/shard_map/panel_product/pallas_call | solution.py:330
  27.0 0.6 %copy.9 = bf16[2,16,512]{2,1,0:T(8,128)(2,1)} copy(bf16[2,16,512]{2,1,0:T(8,128)(2,1)S(1)} %panel_product.1) | data formatting | bytes 65536

commit v4 on v3

--- a/solution.py
+++ b/solution.py
@@ -108,12 +108,14 @@
         return pltpu.make_async_copy(
             vectors_hbm.at[child, pl.ds(group * OWNERS, OWNERS), xx],
             vectors.at[group, child, xx],
-            load_sem.at[group, child, xx],
-        )
+            load_sem.at[group, child],
+        )
+
+    def wait_all(ref, sem):
+        pltpu.make_async_copy(ref, ref, sem).wait()
 
     def wait_loads(group, child):
-        for xx in range(NX):
-            load(group, child, xx).wait()
+        wait_all(vectors.at[group, child], load_sem.at[group, child])
 
     def start_loads(group, child):
         for xx in range(NX):
@@ -180,8 +182,8 @@
         return remote(
             part.at[group, child, side, x_peers[n]],
             arrived.at[group, child, side, n],
-            x_send.at[group, child, side, n],
-            x_recv.at[group, child, side, n],
+            x_send,
+            x_recv.at[group, child, side],
             at(z, x_peers[n]),
         )
 
@@ -193,15 +195,15 @@
         return remote(
             spread.at[child, side, z_peers[n]],
             landed.at[child, side, n],
-            z_send.at[child, side, n],
-            z_recv.at[child, side, n],
+            z_send,
+            z_recv.at[child, side],
             at(z_peers[n], x),
         )
 
     def send_z(group, child, side):
         total = part[group, child, side, x].astype(jnp.float32)
+        wait_all(arrived.at[group, child, side], x_recv.at[group, child, side])
         for n in range(NX - 1):
-            x_copy(group, child, side, n).wait_recv()
             total = total + arrived[group, child, side, n].astype(jnp.float32)
         spread[child, side, pl.ds(group * OWNERS, OWNERS)] = total.astype(jnp.bfloat16)
         for n, zz in enumerate(z_peers):
@@ -211,10 +213,10 @@
                 z_copy(child, side, n).start()
 
     def tx_copy(n):
-        return remote(own_total, x_totals.at[n], tx_send.at[n], tx_recv.at[n], at(z, x_peers[n]))
+        return remote(own_total, x_totals.at[n], tx_send, tx_recv, at(z, x_peers[n]))
 
     def tz_copy(n):
-        return remote(z_own, z_totals.at[n], tz_send.at[n], tz_recv.at[n], at(z_peers[n], x))
+        return remote(z_own, z_totals.at[n], tz_send, tz_recv, at(z_peers[n], x))
 
     def loop(count):
         def run(body):
@@ -279,8 +281,7 @@
 
         @pl.when(step == 1)
         def _():
-            for n in range(NX - 1):
-                tx_copy(n).wait_recv()
+            wait_all(x_totals, tx_recv)
             z_own[...] = own_total[...] + x_totals[0] + x_totals[1] + x_totals[2]
             for n in range(NZ - 1):
                 tz_copy(n).start()
@@ -288,8 +289,8 @@
         send_z(group, child, side)
 
     total = z_own[...]
+    wait_all(z_totals, tz_recv)
     for n in range(NZ - 1):
-        tz_copy(n).wait_recv()
         total = total + z_totals[n]
     scale[...] = lax.rsqrt(total)
 
@@ -297,8 +298,8 @@
     def _(unit):
         child, side = unit // 2, unit % 2
         result = spread[child, side, z].astype(jnp.float32)
+        wait_all(landed.at[child, side], z_recv.at[child, side])
         for n in range(NZ - 1):
-            z_copy(child, side, n).wait_recv()
             result = result + landed[child, side, n].astype(jnp.float32)
         for block in range(2):
             first = pl.multiple_of(side * WIDTH + block * 128, 128)
@@ -306,19 +307,10 @@
                 result[:, block * 128 : block * 128 + 128] * scale[pl.ds(side * 2 + block, 1)]
             ).astype(jnp.bfloat16)
 
-    @loop(4)
-    def _(unit):
-        child, side = unit // 2, unit % 2
-        for n in range(NX - 1):
-            x_copy(0, child, side, n).wait_send()
-            x_copy(1, child, side, n).wait_send()
-        for n in range(NZ - 1):
-            z_copy(child, side, n).wait_send()
-
-    for n in range(NX - 1):
-        tx_copy(n).wait_send()
-    for n in range(NZ - 1):
-        tz_copy(n).wait_send()
+    wait_all(arrived, x_send)
+    wait_all(landed, z_send)
+    wait_all(x_totals, tx_send)
+    wait_all(z_totals, tz_send)
 
 
 def local(child_vectors, merge_position, pole_frac, weights, retained, root_index, root_offset):
@@ -356,15 +348,15 @@
             pltpu.SemaphoreType.REGULAR,
             pltpu.SemaphoreType.REGULAR,
             dma((6,)),
-            dma((2, children, NX)),
-            dma((2, children, sides, NX - 1)),
-            dma((2, children, sides, NX - 1)),
-            dma((children, sides, NZ - 1)),
-            dma((children, sides, NZ - 1)),
-            dma((NX - 1,)),
-            dma((NX - 1,)),
-            dma((NZ - 1,)),
-            dma((NZ - 1,)),
+            dma((2, children)),
+            dma,
+            dma((2, children, sides)),
+            dma,
+            dma((children, sides)),
+            dma,
+            dma,
+            dma,
+            dma,
         ],
         compiler_params=pltpu.CompilerParams(
             collective_id=0, has_side_effects=True, vmem_limit_bytes=24 * 2**20

time: 27.7 us -> 26.5 us (0.957)
  Pallas kernels: 27 us -> 25.8 us
    pallas_call x1, Pallas kernels: 27 us -> 25.8 us  [local(): pl.pallas_call(kernel, out_shape=jax.ShapeDtypeStruct((children, 16, cols...]
where the time goes in v4:
time: 26.5 us; the launch traced here: 26.4 us
  Pallas kernels  25.8 us (97%)
  local copies, waits for them, and re-layouts  0.62 us (2%)
    pallas_call x1, Pallas kernels, local(): pl.pallas_call(kernel, out_shape=jax.ShapeDtypeStruct((children, 16, cols...  25.8 us
    unnamed x1, local copies, waits for them, and re-layouts  0.62 us

profile of v4, /device:TPU:1, one launch (start us, length us, event | category | flops | bytes accessed | tf_op | source)
XLA Modules:
  0.0 26.4 jit_solution(12476056041730016082)
XLA Ops:
  0.0 25.8 %panel_product.1 = bf16[2,16,512]{2,1,0:T(8,128)(2,1)S(1)} custom-call(bf16[2,8,4,16,2048]{4,3,2,1,0:T(8,128)(2,1)} %bitcast.3, s32[2,2048]{1,0:T(2,128)} %position_hbm.1, f32[2,2048]{1,0:T(2,128)} %fraction_hbm.1, f32[2,2048]{1,0:T(2,128)} %weight_hbm.1, s32[2,2048]{1,0:T(2,128)} %keep_hbm.1, s32[1,512]{1,0:T(1,128)} %bitcast.4, f32[1,512]{1,0:T(1,128)} %bitcast.5), custom_call_target="tpu_custom_call" | custom-call | tf_op jit(solution)/shard_map/panel_product/pallas_call | solution.py:322
  25.8 0.6 %copy.9 = bf16[2,16,512]{2,1,0:T(8,128)(2,1)} copy(bf16[2,16,512]{2,1,0:T(8,128)(2,1)S(1)} %panel_product.1) | data formatting | bytes 65536

commit v5 on v4

--- a/solution.py
+++ b/solution.py
@@ -70,17 +70,18 @@
         small.append(copy)
 
     col = lax.axis_index("col")
-    z = col // NX
-    x = col % NX
+    z = lax.div(col, NX)
+    x = lax.rem(col, NX)
 
     def at(zz, xx):
         return {"col": zz * NX + xx}
 
-    x_peers = [(x + d) % NX for d in (2, 1, 3)]
-    z_peers = [(z + d) % NZ for d in (4, 3, 5, 2, 6, 1, 7)]
-
-    hub_x = 3 - (z // 6 - z // 7)
-    hub_z = 7 - x // 3
+    x_peers = [lax.rem(x + d, NX) for d in (2, 1, 3)]
+    z_peers = [lax.rem(z + d, NZ) for d in (4, 3, 5, 2, 6, 1, 7)]
+
+    hub_x = 3 - (lax.div(z, 6) - lax.div(z, 7))
+    hub_z = 7 - lax.div(x, 3)
+    half_z = lax.div(z, OWNERS)
     barrier = pltpu.get_barrier_semaphore()
 
     @pl.when(x != hub_x)
@@ -191,26 +192,32 @@
         for n in range(NX - 1):
             x_copy(group, child, side, n).start()
 
-    def z_copy(child, side, n):
-        return remote(
-            spread.at[child, side, z_peers[n]],
-            landed.at[child, side, n],
-            z_send,
-            z_recv.at[child, side],
-            at(z_peers[n], x),
-        )
-
-    def send_z(group, child, side):
+    def send_z(group, child, side, total):
+        owners = pl.ds(group * OWNERS, OWNERS)
+        spread[child, side, owners] = total.astype(jnp.bfloat16)
+        for n in range(OWNERS):
+            zz = group * OWNERS + n
+
+            @pl.when(zz != z)
+            def _(zz=zz):
+                remote(
+                    spread.at[child, side, zz],
+                    landed.at[child, side, z],
+                    z_send,
+                    z_recv.at[child, side],
+                    at(zz, x),
+                ).start()
+
+        @pl.when(half_z == group)
+        def _():
+            landed[child, side, z] = spread[child, side, z]
+
+    def gather(group, child, side):
         total = part[group, child, side, x].astype(jnp.float32)
         wait_all(arrived.at[group, child, side], x_recv.at[group, child, side])
         for n in range(NX - 1):
             total = total + arrived[group, child, side, n].astype(jnp.float32)
-        spread[child, side, pl.ds(group * OWNERS, OWNERS)] = total.astype(jnp.bfloat16)
-        for n, zz in enumerate(z_peers):
-
-            @pl.when(zz // OWNERS == group)
-            def _(n=n):
-                z_copy(child, side, n).start()
+        send_z(group, child, side, total)
 
     def tx_copy(n):
         return remote(own_total, x_totals.at[n], tx_send, tx_recv, at(z, x_peers[n]))
@@ -272,7 +279,7 @@
         def _():
             pl.semaphore_wait(z_ready, 1)
 
-        send_z(0, 0, child)
+        gather(0, 0, child)
 
     @loop(6)
     def _(step):
@@ -286,7 +293,7 @@
             for n in range(NZ - 1):
                 tz_copy(n).start()
 
-        send_z(group, child, side)
+        gather(group, child, side)
 
     total = z_own[...]
     wait_all(z_totals, tz_recv)
@@ -297,9 +304,9 @@
     @loop(4)
     def _(unit):
         child, side = unit // 2, unit % 2
-        result = spread[child, side, z].astype(jnp.float32)
-        wait_all(landed.at[child, side], z_recv.at[child, side])
-        for n in range(NZ - 1):
+        wait_all(landed.at[child, side, pl.ds(0, NZ - 1)], z_recv.at[child, side])
+        result = landed[child, side, 0].astype(jnp.float32)
+        for n in range(1, NZ):
             result = result + landed[child, side, n].astype(jnp.float32)
         for block in range(2):
             first = pl.multiple_of(side * WIDTH + block * 128, 128)
@@ -308,7 +315,7 @@
             ).astype(jnp.bfloat16)
 
     wait_all(arrived, x_send)
-    wait_all(landed, z_send)
+    wait_all(landed.at[:, :, pl.ds(0, NZ - 1)], z_send)
     wait_all(x_totals, tx_send)
     wait_all(z_totals, tz_send)
 
@@ -339,7 +346,7 @@
             pltpu.VMEM((2, children, sides, NX, OWNERS, 16, WIDTH), bf16),
             pltpu.VMEM((2, children, sides, NX - 1, OWNERS, 16, WIDTH), bf16),
             pltpu.VMEM((children, sides, NZ, 16, WIDTH), bf16),
-            pltpu.VMEM((children, sides, NZ - 1, 16, WIDTH), bf16),
+            pltpu.VMEM((children, sides, NZ, 16, WIDTH), bf16),
             pltpu.VMEM((cols // 128, 128), f32),
             pltpu.VMEM((NX - 1, cols // 128, 128), f32),
             pltpu.VMEM((cols // 128, 128), f32),

time: 26.5 us -> 25.7 us (0.970)
  the two profiles are of different devices: /device:TPU:1 before, /device:TPU:56 now
where the time goes in v5:
time: 25.7 us; the launch traced here: 25.4 us
  Pallas kernels  24.8 us (96%)
  local copies, waits for them, and re-layouts  0.62 us (2%)
    pallas_call x1, Pallas kernels, local(): pl.pallas_call(kernel, out_shape=jax.ShapeDtypeStruct((children, 16, cols...  24.8 us
    unnamed x1, local copies, waits for them, and re-layouts  0.62 us

profile of v5, /device:TPU:56, one launch (start us, length us, event | category | flops | bytes accessed | tf_op | source)
XLA Modules:
  0.0 25.4 jit_solution(13877170070482384264)
XLA Ops:
  0.0 24.8 %panel_product.1 = bf16[2,16,512]{2,1,0:T(8,128)(2,1)S(1)} custom-call(bf16[2,8,4,16,2048]{4,3,2,1,0:T(8,128)(2,1)} %bitcast.3, s32[2,2048]{1,0:T(2,128)} %position_hbm.1, f32[2,2048]{1,0:T(2,128)} %fraction_hbm.1, f32[2,2048]{1,0:T(2,128)} %weight_hbm.1, s32[2,2048]{1,0:T(2,128)} %keep_hbm.1, s32[1,512]{1,0:T(1,128)} %bitcast.4, f32[1,512]{1,0:T(1,128)} %bitcast.5), custom_call_target="tpu_custom_call" | custom-call | tf_op jit(solution)/shard_map/panel_product/pallas_call | solution.py:329
  24.8 0.6 %copy.9 = bf16[2,16,512]{2,1,0:T(8,128)(2,1)} copy(bf16[2,16,512]{2,1,0:T(8,128)(2,1)S(1)} %panel_product.1) | data formatting | bytes 65536

commit v6 on v5

--- a/solution.py
+++ b/solution.py
@@ -266,6 +266,12 @@
 
         send_x(0, child, side)
 
+    @pl.when(z != hub_z)
+    def _():
+        pl.semaphore_wait(z_ready, 1)
+
+    gather(0, 0, 0)
+
     @loop(2)
     def _(child):
         wait_loads(1, child)
@@ -275,11 +281,10 @@
         for side in range(2):
             send_x(1, child, side)
 
-        @pl.when(jnp.logical_and(child == 0, z != hub_z))
-        def _():
-            pl.semaphore_wait(z_ready, 1)
-
-        gather(0, 0, child)
+
+        @pl.when(child == 0)
+        def _():
+            gather(0, 0, 1)
 
     @loop(6)
     def _(step):

time: 25.7 us -> 25.1 us (0.977)
  Pallas kernels: 24.8 us -> 24.3 us
    pallas_call x1, Pallas kernels: 24.8 us -> 24.3 us  [local(): pl.pallas_call(kernel, out_shape=jax.ShapeDtypeStruct((children, 16, cols...]
where the time goes in v6:
time: 25.1 us; the launch traced here: 25 us
  Pallas kernels  24.3 us (97%)
  local copies, waits for them, and re-layouts  0.62 us (2%)
    pallas_call x1, Pallas kernels, local(): pl.pallas_call(kernel, out_shape=jax.ShapeDtypeStruct((children, 16, cols...  24.3 us
    unnamed x1, local copies, waits for them, and re-layouts  0.62 us

profile of v6, /device:TPU:56, one launch (start us, length us, event | category | flops | bytes accessed | tf_op | source)
XLA Modules:
  0.0 25.0 jit_solution(9567788391550721679)
XLA Ops:
  0.0 24.3 %panel_product.1 = bf16[2,16,512]{2,1,0:T(8,128)(2,1)S(1)} custom-call(bf16[2,8,4,16,2048]{4,3,2,1,0:T(8,128)(2,1)} %bitcast.3, s32[2,2048]{1,0:T(2,128)} %position_hbm.1, f32[2,2048]{1,0:T(2,128)} %fraction_hbm.1, f32[2,2048]{1,0:T(2,128)} %weight_hbm.1, s32[2,2048]{1,0:T(2,128)} %keep_hbm.1, s32[1,512]{1,0:T(1,128)} %bitcast.4, f32[1,512]{1,0:T(1,128)} %bitcast.5), custom_call_target="tpu_custom_call" | custom-call | tf_op jit(solution)/shard_map/panel_product/pallas_call | solution.py:334
  24.3 0.6 %copy.9 = bf16[2,16,512]{2,1,0:T(8,128)(2,1)} copy(bf16[2,16,512]{2,1,0:T(8,128)(2,1)S(1)} %panel_product.1) | data formatting | bytes 65536

commit v7 on v6

--- a/solution.py
+++ b/solution.py
@@ -34,6 +34,8 @@
     squares,
     part,
     arrived,
+    ring,
+    sent,
     spread,
     landed,
     own_total,
@@ -47,6 +49,8 @@
     load_sem,
     x_send,
     x_recv,
+    r_send,
+    r_recv,
     z_send,
     z_recv,
     tx_send,
@@ -184,7 +188,7 @@
             part.at[group, child, side, x_peers[n]],
             arrived.at[group, child, side, n],
             x_send,
-            x_recv.at[group, child, side],
+            x_recv.at[child, side],
             at(z, x_peers[n]),
         )
 
@@ -214,10 +218,45 @@
 
     def gather(group, child, side):
         total = part[group, child, side, x].astype(jnp.float32)
-        wait_all(arrived.at[group, child, side], x_recv.at[group, child, side])
+        wait_all(arrived.at[group, child, side], x_recv.at[child, side])
         for n in range(NX - 1):
             total = total + arrived[group, child, side, n].astype(jnp.float32)
         send_z(group, child, side, total)
+
+    def ring_copy(child, side, d, step):
+        beside = x_peers[1 + d]
+        owners = pl.ds((1 - d if step == 1 else d) * 2, 2)
+        return remote(
+            (
+                part.at[1, child, side, x_peers[0], owners],
+                part.at[1, child, side, beside, owners],
+                sent.at[child, side, d],
+            )[step],
+            ring.at[child, side, d] if step == 0 else arrived.at[1, child, side, d, owners],
+            r_send,
+            r_recv.at[min(step, 1), child, side],
+            at(z, beside),
+        )
+
+    def send_ring(child, side, step):
+        for d in range(2):
+            ring_copy(child, side, d, step).start()
+
+    def pass_ring(child, side):
+        wait_all(ring.at[child, side], r_recv.at[0, child, side])
+        for d in range(2):
+            sent[child, side, d] = (
+                part[1, child, side, x_peers[1 + d], pl.ds(d * 2, 2)].astype(jnp.float32)
+                + ring[child, side, d].astype(jnp.float32)
+            ).astype(jnp.bfloat16)
+        send_ring(child, side, 2)
+
+    def gather_ring(child, side):
+        total = part[1, child, side, x].astype(jnp.float32)
+        wait_all(arrived.at[1, child, side, pl.ds(0, 2)], r_recv.at[1, child, side])
+        for d in range(2):
+            total = total + arrived[1, child, side, d].astype(jnp.float32)
+        send_z(1, child, side, total)
 
     def tx_copy(n):
         return remote(own_total, x_totals.at[n], tx_send, tx_recv, at(z, x_peers[n]))
@@ -279,26 +318,31 @@
         for side in range(2):
             part[1, child, side] = block[:, side * WIDTH : side * WIDTH + WIDTH].reshape(NX, OWNERS, 16, WIDTH)
         for side in range(2):
-            send_x(1, child, side)
+            send_ring(child, side, 0)
 
 
         @pl.when(child == 0)
         def _():
             gather(0, 0, 1)
 
-    @loop(6)
-    def _(step):
-        unit = step + 2
-        group, child, side = unit // 4, unit // 2 % 2, unit % 2
-
-        @pl.when(step == 1)
-        def _():
-            wait_all(x_totals, tx_recv)
-            z_own[...] = own_total[...] + x_totals[0] + x_totals[1] + x_totals[2]
-            for n in range(NZ - 1):
-                tz_copy(n).start()
-
-        gather(group, child, side)
+    @loop(4)
+    def _(unit):
+        send_ring(lax.div(unit, 2), lax.rem(unit, 2), 1)
+
+    gather(0, 1, 0)
+    wait_all(x_totals, tx_recv)
+    z_own[...] = own_total[...] + x_totals[0] + x_totals[1] + x_totals[2]
+    for n in range(NZ - 1):
+        tz_copy(n).start()
+    gather(0, 1, 1)
+
+    @loop(4)
+    def _(unit):
+        pass_ring(lax.div(unit, 2), lax.rem(unit, 2))
+
+    @loop(4)
+    def _(unit):
+        gather_ring(lax.div(unit, 2), lax.rem(unit, 2))
 
     total = z_own[...]
     wait_all(z_totals, tz_recv)
@@ -319,7 +363,8 @@
                 result[:, block * 128 : block * 128 + 128] * scale[pl.ds(side * 2 + block, 1)]
             ).astype(jnp.bfloat16)
 
-    wait_all(arrived, x_send)
+    wait_all(arrived.at[0], x_send)
+    wait_all(part.at[1, :, :, pl.ds(0, 3)], r_send)
     wait_all(landed.at[:, :, pl.ds(0, NZ - 1)], z_send)
     wait_all(x_totals, tx_send)
     wait_all(z_totals, tz_send)
@@ -350,6 +395,8 @@
             pltpu.VMEM((cols // 8, 8, 128), f32),
             pltpu.VMEM((2, children, sides, NX, OWNERS, 16, WIDTH), bf16),
             pltpu.VMEM((2, children, sides, NX - 1, OWNERS, 16, WIDTH), bf16),
+            pltpu.VMEM((children, sides, 2, OWNERS // 2, 16, WIDTH), bf16),
+            pltpu.VMEM((children, sides, 2, OWNERS // 2, 16, WIDTH), bf16),
             pltpu.VMEM((children, sides, NZ, 16, WIDTH), bf16),
             pltpu.VMEM((children, sides, NZ, 16, WIDTH), bf16),
             pltpu.VMEM((cols // 128, 128), f32),
@@ -361,6 +408,8 @@
             pltpu.SemaphoreType.REGULAR,
             dma((6,)),
             dma((2, children)),
+            dma,
+            dma((children, sides)),
             dma,
             dma((2, children, sides)),
             dma,

time: 25.1 us -> 24.9 us (level)
  no operation moved by 1% of the time
where the time goes in v7:
time: 24.9 us; the launch traced here: 24.8 us
  Pallas kernels  24.2 us (97%)
  local copies, waits for them, and re-layouts  0.62 us (2%)
    pallas_call x1, Pallas kernels, local(): pl.pallas_call(kernel, out_shape=jax.ShapeDtypeStruct((children, 16, cols...  24.2 us
    unnamed x1, local copies, waits for them, and re-layouts  0.62 us

profile of v7, /device:TPU:56, one launch (start us, length us, event | category | flops | bytes accessed | tf_op | source)
XLA Modules:
  0.0 24.8 jit_solution(992989853256215777)
XLA Ops:
  0.0 24.2 %panel_product.1 = bf16[2,16,512]{2,1,0:T(8,128)(2,1)S(1)} custom-call(bf16[2,8,4,16,2048]{4,3,2,1,0:T(8,128)(2,1)} %bitcast.3, s32[2,2048]{1,0:T(2,128)} %position_hbm.1, f32[2,2048]{1,0:T(2,128)} %fraction_hbm.1, f32[2,2048]{1,0:T(2,128)} %weight_hbm.1, s32[2,2048]{1,0:T(2,128)} %keep_hbm.1, s32[1,512]{1,0:T(1,128)} %bitcast.4, f32[1,512]{1,0:T(1,128)} %bitcast.5), custom_call_target="tpu_custom_call" | custom-call | tf_op jit(solution)/shard_map/panel_product/pallas_call | solution.py:379
  24.2 0.6 %copy.9 = bf16[2,16,512]{2,1,0:T(8,128)(2,1)} copy(bf16[2,16,512]{2,1,0:T(8,128)(2,1)S(1)} %panel_product.1) | data formatting | bytes 65536
